TPU v7x, 128 devices: a whole 4x4x4 slice. The times are simulated.
128 devices in a mesh: slab: 4 (over z_hi, core), wide: 32 (over x, z_lo, y).
Axes of the slice: x: 4, y: 4, z: 4 (z_hi: 2, z_lo: 2; z = z_hi * 2 + z_lo), core: 2. Of those that a mesh axis runs over, the one named last changes fastest.
Arguments:
- orbitals: float32 [256, 128, 128, 128], P(None, 'slab', 'wide'), may hold values from -6 to 6
- points: int32 [512], replicated, may hold values from 0 to 2097151, as said below
Outputs:
- potential: float32 [128, 128, 128, 128], P(None, 'slab', 'wide')
Inputs may be any that keep to these rules, and one draw needn't show every extreme that they name: `points`: the 512 indices are distinct; how many fall in the cells of one device differs strongly between devices.
All inputs are finite; a program needn't handle non-finite values.
Results may differ from a plain program's by a relative error of at most 0.00014.
Values sent between devices are 32-bit elements; how exact they have to be, the bound alone decides.
No kernel may reach another device: no remote copies, remote signals or barrier semaphores. Data moves between devices by JAX's collectives and lax.ppermute only.
A program may use at most 192 MiB of HBM per device.

v0:
```python
import math
import jax
import jax.numpy as jnp
from jax import lax
from jax.sharding import PartitionSpec as P

VEC_DEV = 1
highest = lax.Precision.HIGHEST


def tables(length):
    index = jnp.arange(length, dtype=jnp.int32)
    phase = index[:, None] * index[None, :] % length
    angle = phase.astype(jnp.float32) * (2.0 * math.pi / length)
    return (jnp.cos(angle), jnp.sin(angle))


def contract(values, table, axis_pos):
    letters = "abcd"[: values.ndim]
    target = letters[:axis_pos] + "k" + letters[axis_pos + 1 :]
    return jnp.einsum(
        letters + "," + letters[axis_pos] + "k->" + target, values, table, precision=highest
    )


def rotate(stacked, axis_pos, sign, cosine, sine):
    real_part = stacked[0]
    imag_part = stacked[1]
    new_real = contract(real_part, cosine, axis_pos) - sign * contract(imag_part, sine, axis_pos)
    new_imag = contract(imag_part, cosine, axis_pos) + sign * contract(real_part, sine, axis_pos)
    return jnp.stack([new_real, new_imag])


def coulomb(zfreq, yfreq, xfreq, length, factor):

    def squared(index):
        signed = jnp.where(index > length // 2, index - length, index).astype(jnp.float32) * (
            2.0 * math.pi / length
        )
        return signed * signed

    total = (
        squared(zfreq)[:, None, None]
        + squared(yfreq)[None, :, None]
        + squared(xfreq)[None, None, :]
    )
    safe = jnp.where(total > 0, total, 1.0)
    return jnp.where(total > 0, 4.0 * math.pi * factor / safe, 0.0)


def per_device(orbitals, points):
    norbit, depth, rows, grid = orbitals.shape
    npoint = points.shape[0]
    slab_count = lax.axis_size("slab")
    wide_count = lax.axis_size("wide")
    slab_index = lax.axis_index("slab")
    wide_index = lax.axis_index("wide")
    cells = depth * rows * grid
    flat = orbitals.reshape(norbit, cells)
    zcoord = points // (grid * grid)
    ycoord = points // grid % grid
    xcoord = points % grid
    owned = (zcoord // depth == slab_index) & (ycoord // rows == wide_index)
    offset = ((zcoord - slab_index * depth) * rows + (ycoord - wide_index * rows)) * grid + xcoord
    offset = jnp.where(owned, offset, 0)
    picked = jnp.take(flat, offset, axis=1) * owned.astype(jnp.float32)[None, :]
    sampled = lax.psum(picked, ("slab", "wide"))
    correlation = jnp.dot(sampled.T, sampled, precision=highest)
    gram = correlation * correlation
    gram = gram + 0.01 * jnp.mean(jnp.diagonal(gram)) * jnp.eye(npoint, dtype=jnp.float32)
    factor = jnp.linalg.cholesky(gram)
    devices = slab_count * wide_count
    vectors = VEC_DEV * devices
    coeffs = jax.scipy.linalg.cho_solve((factor, True), jnp.eye(npoint, vectors, dtype=jnp.float32))
    coeff_rows = coeffs.T
    sampled_rows = sampled.T
    width = math.gcd(cells, 4096)

    def fit_block(turn, fitted):
        start = turn * width
        block = lax.dynamic_slice_in_dim(flat, start, width, 1)
        pairs = jnp.dot(sampled_rows, block, precision=highest)
        piece = jnp.dot(coeff_rows, pairs * pairs, precision=highest)
        return lax.dynamic_update_slice_in_dim(fitted, piece, start, 1)

    fitting = lax.fori_loop(0, cells // width, fit_block, jnp.zeros((vectors, cells), jnp.float32))
    cosine, sine = tables(grid)
    scale = 1.0 / float(grid * grid * grid)
    freqs = jnp.arange(grid, dtype=jnp.int32)
    stacked = fitting.reshape(2, vectors // 2, depth, rows, grid)
    spectrum = rotate(stacked, 3, -1.0, cosine, sine)
    spectrum = lax.all_to_all(spectrum, "wide", split_axis=1, concat_axis=3, tiled=True)
    spectrum = rotate(spectrum, 2, -1.0, cosine, sine)
    spectrum = lax.all_to_all(spectrum, "slab", split_axis=3, concat_axis=2, tiled=True)
    spectrum = rotate(spectrum, 1, -1.0, cosine, sine)
    block = grid // slab_count
    kernel = coulomb(
        freqs, slab_index * block + jnp.arange(block, dtype=jnp.int32), freqs, grid, scale
    )
    spectrum = spectrum * kernel
    spectrum = rotate(spectrum, 1, 1.0, cosine, sine)
    spectrum = lax.all_to_all(spectrum, "slab", split_axis=2, concat_axis=3, tiled=True)
    spectrum = rotate(spectrum, 2, 1.0, cosine, sine)
    spectrum = lax.all_to_all(spectrum, "wide", split_axis=3, concat_axis=1, tiled=True)
    spectrum = rotate(spectrum, 3, 1.0, cosine, sine)
    return spectrum.reshape(vectors, depth, rows, grid)


def solution(mesh):
    placed = (P(None, "slab", "wide", None), P())
    return jax.shard_map(
        per_device,
        mesh=mesh,
        in_specs=placed,
        out_specs=P(None, "slab", "wide", None),
        check_vma=False,
    )
```

profile of v0, /device:TPU:0, one launch (start us, length us, event | category | flops | bytes accessed | tf_op | source)
XLA Modules:
  0.0 1024.6 jit_solution(7619435522696950387)
XLA Ops:
  7.3 19.6 %copy.67 = f32[256,32,4,128]{0,3,2,1:T(8,128)} copy(f32[256,32,4,128]{3,2,1,0:T(4,128)} %param.4) | data formatting | bytes 33554432 | tf_op args[0]
  26.9 7.3 gather_fusion
  35.3 148.4 %all-reduce.3.cloned.1.call-done = f32[256,512]{0,1:T(8,128)} async-done(((f32[256,512]{0,1:T(8,128)}), f32[256,512]{0,1:T(8,128)}) %all-reduce.3.cloned.1.call-update) | async-done | bytes 524304 | tf_op jit(solution)/shard_map/psum | solution.py:67
  183.7 2.2 convolution_multiply_fusion
  186.3 5.0 gather_fusion.1
  192.9 11.7 %cholesky.103 = f32[128,128]{1,0:T(8,128)S(1)} custom-call(f32[128,128]{1,0:T(8,128)S(1)} %cholesky.263), custom_call_target="Cholesky" | custom-call | tf_op jit(solution)/shard_map/jit(cholesky)/cholesky | solution.py:71
  204.7 9.8 custom-call.34
  215.2 11.7 %cholesky.215 = f32[128,128]{1,0:T(8,128)S(1)} custom-call(f32[128,128]{1,0:T(8,128)S(1)} %cholesky.267), custom_call_target="Cholesky" | custom-call | tf_op jit(solution)/shard_map/jit(cholesky)/cholesky | solution.py:71
  227.0 9.9 custom-call.35
  237.6 11.7 %cholesky.236 = f32[128,128]{1,0:T(8,128)S(1)} custom-call(f32[128,128]{1,0:T(8,128)S(1)} %cholesky.272), custom_call_target="Cholesky" | custom-call | tf_op jit(solution)/shard_map/jit(cholesky)/cholesky | solution.py:71
  250.0 9.8 custom-call.36
  260.5 11.7 %cholesky.253 = f32[128,128]{1,0:T(8,128)S(1)} custom-call(f32[128,128]{1,0:T(8,128)S(1)} %convolution_subtract_fusion.8), custom_call_target="Cholesky" | custom-call | tf_op jit(solution)/shard_map/jit(cholesky)/cholesky | solution.py:71
  276.3 10.6 %while.15 = (s32[]{:T(128)}, f32[512,512]{1,0:T(8,128)S(1)}, s32[4,2]{0,1:T(2,128)S(1)}, f32[4,128,128]{2,1,0:T(8,128)}, s32[]{:T(128)}) while((s32[]{:T(128)}, f32[512,512]{1,0:T(8,128)S(1)}, s32[4,2]{0,1:T(2,128)S(1)}, f32[4,128,128]{2,1,0:T(8,128)}, s32[]{:T(128)}) %tuple.60), condition=%wide.while_cond, body=%wide.while_body.sunk | while | flops 2 | bytes 132705 | solution.py:74
  286.8 40.3 %custom-call.37 = f32[4,128,128]{1,2,0:T(8,128)S(1)} custom-call(f32[4,128,128]{2,1,0:T(8,128)} %get-tuple-element.107), custom_call_target="InvertDiagBlocksLowerTriangular" | custom-call | tf_op jit(solution)/shard_map/jit(_cho_solve)/triangular_solve | solution.py:74
  331.3 3.7 broadcast_in_dim.35
  335.0 68.7 %while.14 = (s32[]{:T(128)}, f32[128,16384]{0,1:T(8,128)}, f32[256,16384]{0,1:T(8,128)}, f32[512,256]{1,0:T(8,128)S(1)}, f32[128,512]{1,0:T(8,128)S(1)}, /*index=5*/s32[]{:T(128)}, s32[]{:T(128)}, s32[]{:T(128)}, s32[]{:T(128)}) while((s32[]{:T(128)}, f32[128,16384]{0,1:T(8,128)}, f32[256,16384]{0,1:T(8,128)}, f32[512,256]{1,0:T(8,128)S(1)}, ...), condition=%wide.region_11.12_spmd, body=%wide.region_10.11_spmd.sunk | while | flops 9665773568 | bytes 23855252 | solution.py:86
  335.0 9.1 fusion.295
  344.1 8.1 fusion.296
  352.2 9.1 fusion.295
  361.3 8.1 fusion.296
  369.3 9.1 fusion.295
  378.4 8.1 fusion.296
  386.5 9.1 fusion.295
  395.6 8.1 fusion.296
  403.7 13.2 %fusion.249 = (f32[64,16384]{0,1:T(8,128)}, f32[64,16384]{0,1:T(8,128)}) fusion(f32[128,16384]{0,1:T(8,128)} %get-tuple-element.99), kind=kLoop, calls=%fused_computation.325 | loop fusion | bytes 16777216 | tf_op jit(solution)/shard_map/slice | solution.py:27
  416.9 7.3 copy.72
  424.2 7.1 fusion.79
  431.3 7.3 copy.74
  438.7 7.4 fusion.77
  446.0 3.9 subtract_bitcast_fusion.5
  450.0 3.9 add_bitcast_fusion.5
  457.7 101.2 %all_to_all.60 = f32[2,64,32,4,128]{4,2,3,0,1:T(8,128)} all-to-all(f32[2,64,32,4,128]{4,2,3,0,1:T(8,128)S(1)} %copy.77), channel_id=1, replica_groups=mesh['slab'=4,'wide'=32] {'wide'}, dimensions={1} | all-to-all | bytes 16777216 | tf_op jit(solution)/shard_map/all_to_all | solution.py:92
  558.9 12.2 %copy.150 = f32[2,32,2,32,4,128]{5,4,1,3,2,0:T(4,128)} copy(f32[2,32,2,32,4,128]{5,3,4,0,2,1:T(8,128)} %bitcast.268) | data formatting | bytes 16777216 | tf_op jit(solution)/shard_map/all_to_all | solution.py:92
  571.1 4.0 fusion.248
  575.1 4.1 fusion.81
  579.2 4.5 fusion.71
  583.7 4.3 subtract_bitcast_fusion.4
  588.0 4.3 add_bitcast_fusion.4
  593.3 8.4 copy.83
  601.8 5.7 all-to-all-start.1
  608.2 93.9 %all-to-all-done.1 = f32[2,2,32,128,128]{4,2,1,0,3:T(8,128)} async-done(((f32[2,2,32,128,128]{4,2,1,0,3:T(8,128)}), f32[2,2,32,128,128]{4,2,1,0,3:T(8,128)}, u32[]{:S(2)}, u32[]{:S(2)}) %all-to-all-start.1) | async-done | bytes 8388640 | tf_op jit(solution)/shard_map/all_to_all | solution.py:94
  702.1 4.4 copy.149
  708.3 4.1 fusion.83
  712.4 4.1 fusion.69
  716.5 5.1 subtract_bitcast_fusion.3
  721.7 4.7 add_bitcast_fusion.3
  727.9 4.4 fusion.12
  732.3 4.4 fusion.11
  736.7 4.6 subtract_bitcast_fusion.2
  741.3 4.4 add_bitcast_fusion.2
  746.9 4.9 copy.93
  751.7 97.3 %all_to_all.61 = f32[2,2,128,32,128]{4,3,1,0,2:T(8,128)S(1)} all-to-all(f32[2,2,128,32,128]{4,3,1,0,2:T(8,128)S(1)} %copy.93), channel_id=1, replica_groups=mesh['slab'=4,'wide'=32] {'slab'}, dimensions={2} | all-to-all | bytes 16777216 | tf_op jit(solution)/shard_map/all_to_all | solution.py:102
  852.4 4.1 fusion.86
  856.5 4.1 fusion.66
  860.6 4.7 subtract_bitcast_fusion.1
  865.3 4.5 add_bitcast_fusion.1
  870.9 5.3 copy.99
  876.2 102.6 %all_to_all.62 = f32[2,2,32,128,128]{4,2,1,0,3:T(8,128)S(1)} all-to-all(f32[2,2,32,128,128]{4,2,1,0,3:T(8,128)S(1)} %copy.99), channel_id=1, replica_groups=mesh['slab'=4,'wide'=32] {'wide'}, dimensions={3} | all-to-all | bytes 16777216 | tf_op jit(solution)/shard_map/all_to_all | solution.py:104
  982.1 3.8 fusion.75
  985.9 3.8 fusion.73
  989.7 4.2 subtract_bitcast_fusion
  993.9 4.0 add_bitcast_fusion
  998.0 4.3 pad_maximum_fusion.4
  1002.3 15.2 %copy.101 = f32[128,32,4,128]{3,2,1,0:T(4,128)} copy(f32[128,32,4,128]{3,1,2,0:T(8,128)} %bitcast.267) | data formatting | bytes 16777216 | tf_op jit(solution)/shard_map/reshape | solution.py:106
  (84 shorter events, 39.5 us)
Async XLA Ops:
  6.5 177.2 %all-reduce.3.cloned.1.call-start = ((), (), s32[]{:S(2)}) async-start(), calls=%async_computation.4 | async-start | bytes 1048576 | tf_op jit(solution)/shard_map/psum | solution.py:67
  331.3 3.7 copy-start.2
  438.6 7.4 copy-start.1
  438.7 7.4 copy-start.3
  446.0 4.0 copy-start
  601.8 100.3 %all-to-all-start.1 = ((f32[2,2,32,128,128]{4,2,1,0,3:T(8,128)}), f32[2,2,32,128,128]{4,2,1,0,3:T(8,128)}, u32[]{:S(2)}, u32[]{:S(2)}) async-start(f32[2,2,32,128,128]{4,2,1,0,3:T(8,128)} %copy.83), calls=%async_computation.1 | async-start | bytes 16777216 | tf_op jit(solution)/shard_map/all_to_all | solution.py:94
Sparse Core Ops, SparseCore 0:
  35.3 148.3 all-reduce.2
where the time goes:
time: 1030 us; the launch traced here: 1020 us
  blocking collectives  301 us (29%)
  waiting for transfers between devices  242 us (23%)
  matrix products  185 us (18%)
  local copies, waits for them, and re-layouts  139 us (13%)
  other arithmetic  133 us (13%)
  between operations  17.5 us (2%)
    psum x1, waiting for transfers between devices, per_device(): sampled = lax.psum(picked, ('slab', 'wide'))  148 us
    dot_general x24, matrix products, contract(): jnp.einsum(letters + ',' + letters[axis_pos] + 'k->' + target, values, ta...  109 us
    all_to_all x1, blocking collectives, per_device(): lax.all_to_all(spectrum, 'wide', split_axis=3, concat_axis=1, tiled=True)  103 us
    all_to_all x1, blocking collectives, per_device(): lax.all_to_all(spectrum, 'wide', split_axis=1, concat_axis=3, tiled=True)  101 us
    all_to_all x1, blocking collectives, per_device(): lax.all_to_all(spectrum, 'slab', split_axis=2, concat_axis=3, tiled=True)  97.3 us
    all_to_all x1, waiting for transfers between devices, per_device(): lax.all_to_all(spectrum, 'slab', split_axis=3, concat_axis=2, tiled=True)  93.9 us
    another operation x14, other arithmetic, per_device(): factor = jnp.linalg.cholesky(gram)  78.6 us
    another operation x3, other arithmetic, per_device(): jax.scipy.linalg.cho_solve((factor, True), jnp.eye(npoint, vectors, dtype...  40.4 us
  transfers between devices with their start and end apart: 2, of which 2 were waited for; matrix products, arithmetic and copies ran while one was open for 0% of the time, Pallas kernels for 0%

commit v1 on v0

--- a/solution.py
+++ b/solution.py
@@ -64,7 +64,8 @@
     offset = ((zcoord - slab_index * depth) * rows + (ycoord - wide_index * rows)) * grid + xcoord
     offset = jnp.where(owned, offset, 0)
     picked = jnp.take(flat, offset, axis=1) * owned.astype(jnp.float32)[None, :]
-    sampled = lax.psum(picked, ("slab", "wide"))
+    parts = lax.all_gather(picked, ("slab", "wide"), axis=0, tiled=False)
+    sampled = parts.sum(axis=0)
     correlation = jnp.dot(sampled.T, sampled, precision=highest)
     gram = correlation * correlation
     gram = gram + 0.01 * jnp.mean(jnp.diagonal(gram)) * jnp.eye(npoint, dtype=jnp.float32)

time: 1030 us -> 1290 us (1.25)
  waiting for transfers between devices: 242 us -> 480 us
  other arithmetic: 133 us -> 153 us
    all_gather x0 -> x1, waiting for transfers between devices: none -> 386 us  [per_device(): parts = lax.all_gather(picked, ('slab', 'wide'), axis=0, tiled=False)]
    psum x1 -> x0, waiting for transfers between devices: 148 us -> none  [per_device(): sampled = lax.psum(picked, ('slab', 'wide'))]
    reduce_sum x0 -> x1, other arithmetic: none -> 20.9 us  [per_device(): sampled = parts.sum(axis=0)]
where the time goes in v1:
time: 1290 us; the launch traced here: 1280 us
  waiting for transfers between devices  480 us (37%)
  blocking collectives  300 us (23%)
  matrix products  188 us (15%)
  other arithmetic  153 us (12%)
  local copies, waits for them, and re-layouts  139 us (11%)
  between operations  17.5 us (1%)
    all_gather x1, waiting for transfers between devices, per_device(): parts = lax.all_gather(picked, ('slab', 'wide'), axis=0, tiled=False)  386 us
    dot_general x24, matrix products, contract(): jnp.einsum(letters + ',' + letters[axis_pos] + 'k->' + target, values, ta...  109 us
    all_to_all x1, blocking collectives, per_device(): lax.all_to_all(spectrum, 'wide', split_axis=1, concat_axis=3, tiled=True)  103 us
    all_to_all x1, blocking collectives, per_device(): lax.all_to_all(spectrum, 'wide', split_axis=3, concat_axis=1, tiled=True)  99.2 us
    all_to_all x1, blocking collectives, per_device(): lax.all_to_all(spectrum, 'slab', split_axis=2, concat_axis=3, tiled=True)  97.3 us
    all_to_all x1, waiting for transfers between devices, per_device(): lax.all_to_all(spectrum, 'slab', split_axis=3, concat_axis=2, tiled=True)  93.9 us
    another operation x14, other arithmetic, per_device(): factor = jnp.linalg.cholesky(gram)  78.6 us
    another operation x3, other arithmetic, per_device(): jax.scipy.linalg.cho_solve((factor, True), jnp.eye(npoint, vectors, dtype...  39.7 us
  transfers between devices with their start and end apart: 2, of which 2 were waited for; matrix products, arithmetic and copies ran while one was open for 0% of the time, Pallas kernels for 0%

profile of v1, /device:TPU:0, one launch (start us, length us, event | category | flops | bytes accessed | tf_op | source)
XLA Modules:
  0.0 1281.8 jit_solution(2659419984308550883)
XLA Ops:
  7.3 19.6 %copy.103 = f32[256,32,4,128]{0,3,2,1:T(8,128)} copy(f32[256,32,4,128]{3,2,1,0:T(4,128)} %param.4) | data formatting | bytes 33554432 | tf_op args[0]
  26.8 7.3 gather_fusion
  35.5 385.8 %all-gather.2.cloned.1.call-done = f32[128,256,512]{2,1,0:T(8,128)} async-done(((f32[1,256,512]{2,1,0:T(8,128)}), f32[128,256,512]{2,1,0:T(8,128)}) %all-gather.2.cloned.1.call-update) | async-done | bytes 67108880 | tf_op jit(solution)/shard_map/all_gather | solution.py:67
  421.2 20.9 %reduce_sum.18 = f32[256,512]{1,0:T(8,128)S(1)} reduce(f32[128,256,512]{2,1,0:T(8,128)} %all-gather.2.cloned.1.call-done, f32[]{:T(128)} %constant.289.clone.1), dimensions={0}, to_apply=%region_0.1 | reduce | flops 16646144 | bytes 67633152 | tf_op jit(solution)/shard_map/reduce_sum | solution.py:68
  443.5 5.0 gather_fusion.1
  451.0 11.7 cholesky.103
  462.9 9.8 custom-call.34
  475.2 11.7 cholesky.215
  487.0 10.0 custom-call.35
  498.5 11.7 cholesky.236
  511.0 9.8 custom-call.36
  522.2 11.7 cholesky.253
  538.0 8.5 while.15
  546.5 39.5 %custom-call.37 = f32[4,128,128]{1,2,0:T(8,128)S(1)} custom-call(f32[4,128,128]{2,1,0:T(8,128)S(1)} %get-tuple-element.107), custom_call_target="InvertDiagBlocksLowerTriangular" | custom-call | tf_op jit(solution)/shard_map/jit(_cho_solve)/triangular_solve | solution.py:75
  590.4 3.7 broadcast_in_dim.35
  594.0 68.7 %while.14 = (s32[]{:T(128)}, f32[128,16384]{0,1:T(8,128)}, f32[256,16384]{0,1:T(8,128)}, f32[512,256]{1,0:T(8,128)S(1)}, f32[128,512]{1,0:T(8,128)S(1)}, /*index=5*/s32[]{:T(128)}, s32[]{:T(128)}, s32[]{:T(128)}, s32[]{:T(128)}) while((s32[]{:T(128)}, f32[128,16384]{0,1:T(8,128)}, f32[256,16384]{0,1:T(8,128)}, f32[512,256]{1,0:T(8,128)S(1)}, ...), condition=%wide.region_11.12_spmd, body=%wide.region_10.11_spmd.sunk | while | flops 9665773568 | bytes 23855252 | solution.py:87
  594.0 9.1 fusion.296
  603.1 8.1 fusion.297
  611.2 9.1 fusion.296
  620.3 8.1 fusion.297
  628.4 9.1 fusion.296
  637.5 8.1 fusion.297
  645.5 9.1 fusion.296
  654.6 8.1 fusion.297
  662.7 13.1 %fusion.250 = (f32[64,16384]{0,1:T(8,128)}, f32[64,16384]{0,1:T(8,128)}) fusion(f32[128,16384]{0,1:T(8,128)} %get-tuple-element.99), kind=kLoop, calls=%fused_computation.326 | loop fusion | bytes 16777216 | tf_op jit(solution)/shard_map/slice | solution.py:27
  675.8 7.3 copy.110
  683.2 7.1 fusion.80
  690.3 7.3 copy.112
  697.6 7.3 fusion.78
  705.0 3.9 subtract_bitcast_fusion.5
  708.9 3.9 add_bitcast_fusion.5
  716.6 103.0 %all_to_all.60 = f32[2,64,32,4,128]{4,2,3,0,1:T(8,128)} all-to-all(f32[2,64,32,4,128]{4,2,3,0,1:T(8,128)S(1)} %copy.115), channel_id=1, replica_groups=mesh['slab'=4,'wide'=32] {'wide'}, dimensions={1} | all-to-all | bytes 16777216 | tf_op jit(solution)/shard_map/all_to_all | solution.py:93
  819.6 12.2 copy.188
  831.8 4.0 fusion.249
  835.9 4.0 fusion.82
  839.9 4.5 fusion.72
  844.5 4.3 subtract_bitcast_fusion.4
  848.8 4.3 add_bitcast_fusion.4
  854.1 8.4 copy.121
  862.5 5.7 all-to-all-start.1
  868.9 93.9 %all-to-all-done.1 = f32[2,2,32,128,128]{4,2,1,0,3:T(8,128)} async-done(((f32[2,2,32,128,128]{4,2,1,0,3:T(8,128)}), f32[2,2,32,128,128]{4,2,1,0,3:T(8,128)}, u32[]{:S(2)}, u32[]{:S(2)}) %all-to-all-start.1) | async-done | bytes 8388640 | tf_op jit(solution)/shard_map/all_to_all | solution.py:95
  962.8 4.4 copy.187
  969.1 4.1 fusion.84
  973.2 4.1 fusion.70
  977.3 5.1 subtract_bitcast_fusion.3
  982.4 4.7 add_bitcast_fusion.3
  988.6 4.4 fusion.12
  993.0 4.4 fusion.11
  997.4 4.6 subtract_bitcast_fusion.2
  1002.1 4.4 add_bitcast_fusion.2
  1007.6 4.9 copy.131
  1012.5 97.3 %all_to_all.61 = f32[2,2,128,32,128]{4,3,1,0,2:T(8,128)S(1)} all-to-all(f32[2,2,128,32,128]{4,3,1,0,2:T(8,128)S(1)} %copy.131), channel_id=1, replica_groups=mesh['slab'=4,'wide'=32] {'slab'}, dimensions={2} | all-to-all | bytes 16777216 | tf_op jit(solution)/shard_map/all_to_all | solution.py:103
  1113.1 4.1 fusion.87
  1117.2 4.1 fusion.67
  1121.3 4.7 subtract_bitcast_fusion.1
  1126.0 4.5 add_bitcast_fusion.1
  1131.6 5.3 copy.137
  1136.9 99.2 %all_to_all.62 = f32[2,2,32,128,128]{4,2,1,0,3:T(8,128)S(1)} all-to-all(f32[2,2,32,128,128]{4,2,1,0,3:T(8,128)S(1)} %copy.137), channel_id=1, replica_groups=mesh['slab'=4,'wide'=32] {'wide'}, dimensions={3} | all-to-all | bytes 16777216 | tf_op jit(solution)/shard_map/all_to_all | solution.py:105
  1239.4 3.8 fusion.76
  1243.2 3.8 fusion.74
  1247.0 4.2 subtract_bitcast_fusion
  1251.2 4.0 add_bitcast_fusion
  1255.2 4.3 pad_maximum_fusion.4
  1259.5 15.2 %copy.139 = f32[128,32,4,128]{3,2,1,0:T(4,128)} copy(f32[128,32,4,128]{3,1,2,0:T(8,128)} %bitcast.271) | data formatting | bytes 16777216 | tf_op jit(solution)/shard_map/reshape | solution.py:107
  (87 shorter events, 43.3 us)
Async XLA Ops:
  6.5 414.7 %all-gather.2.cloned.1.call-start = ((), (), s32[]{:S(2)}) async-start(), calls=%async_computation.4 | async-start | bytes 67633152 | tf_op jit(solution)/shard_map/all_gather | solution.py:67
  450.0 1.0 copy-start.3
  697.6 7.4 copy-start.1
  697.6 7.4 copy-start.2
  704.9 4.0 copy-start
  862.5 100.3 %all-to-all-start.1 = ((f32[2,2,32,128,128]{4,2,1,0,3:T(8,128)}), f32[2,2,32,128,128]{4,2,1,0,3:T(8,128)}, u32[]{:S(2)}, u32[]{:S(2)}) async-start(f32[2,2,32,128,128]{4,2,1,0,3:T(8,128)} %copy.121), calls=%async_computation.1 | async-start | bytes 16777216 | tf_op jit(solution)/shard_map/all_to_all | solution.py:95
Sparse Core Ops, SparseCore 0:
  35.5 385.6 all-gather.1
